TPU v7x, 32 devices: a whole 2x2x4 slice. The times are simulated.
32 devices in a mesh: groups: 2 (over x), ta: 4 (over y, core), xy: 4 (over z).
Axes of the slice: x: 2, y: 2, z: 4, core: 2. Of those that a mesh axis runs over, the one named last changes fastest.
Arguments:
- sources: bfloat16 [8, 4, 4, 8, 96, 256], P('groups', 'ta', 'xy'), parts along dimension 0, may hold values from -24 to 24
- coarse_links: bfloat16 [18, 4, 4, 4, 8, 96, 96], P('groups', None, 'ta', 'xy'), parts along dimension 0, may hold values from -0.119628906 to 0.119628906
Outputs:
- solution: float32 [8, 4, 4, 8, 96, 256], P('groups', 'ta', 'xy'), parts along dimension 0
There are 2 independent parts, one for each index of `groups`. A program takes and returns all parts, laid end to end along the dimension named above; each array names one. Nothing has to cross between parts.
All inputs are finite; a program needn't handle non-finite values.
Results may differ from a plain program's by a relative error of at most 0.0019.
The roundings to bfloat16 on the way count: a program that leaves them out, or rounds other values in their place, can miss the bound.
Values may be sent and summed in bfloat16 or wider, within the bound.
A program may use at most 128 MiB of HBM per device.

v0:
```python
import functools

import jax
import jax.numpy as jnp
from jax import lax
from jax.experimental import pallas as pl
from jax.experimental.pallas import tpu as pltpu
from jax.sharding import PartitionSpec as P

mass_term = 2.0
MESH = pl.DeviceIdType.MESH
HI = lax.Precision.HIGHEST
f32 = jnp.float32
bf16 = jnp.bfloat16

HOPS = (("ta", 1), ("ta", -1), ("xy", 1), ("xy", -1))
CHUNKS = 8
EARLY = (2, 2, 3)
SUMS = 4

mul = functools.partial(lax.dot_general, preferred_element_type=f32)
STRAIGHT = (((1,), (0,)), ((), ()))
TURNED = (((0,), (0,)), ((), ()))


def iotas(n):
    return lax.broadcasted_iota(jnp.int32, (n, n), 0), lax.broadcasted_iota(jnp.int32, (n, n), 1)


def piece_rows(rhs, n_ta):
    return -(-(rhs // 2 + 8) // (8 * n_ta)) * 8


def krylov_kernel(sizes, ny, nz, src, links, first_ref, high_ref, low_ref, curvature_ref, fresh_ref,
                  r, lk, halo1, halo3, u_out, u_in, image, rounded, acc, full, normal, residual, gram_ref, cross_ref, work, inverse0,
                  sums, coef, packed, parts, total, planes, whole, local_sem, bulk_send, bulk_recv, sum_send, sum_recv):
    n_ta, n_xy = sizes["ta"], sizes["xy"]
    me = {axis: lax.axis_index(axis) for axis in sizes}
    n, comp, rhs = r.shape
    per = n // CHUNKS
    half = rhs // 2
    rows = piece_rows(rhs, n_ta)

    def peer(axis, off):
        return lax.rem(me[axis] + off + sizes[axis], sizes[axis])

    def sites(c):
        return pl.ds(c * per, per)

    def vector_copy(stage, d, c, source, halo):
        axis, step = HOPS[d]
        return pltpu.make_async_remote_copy(
            src_ref=source.at[sites(c)], dst_ref=halo.at[d, sites(c)],
            send_sem=bulk_send.at[stage, d, c], recv_sem=bulk_recv.at[stage, d, c],
            device_id={axis: peer(axis, -step)}, device_id_type=MESH)

    def product_copy(d, c):
        axis, step = HOPS[d]
        return pltpu.make_async_remote_copy(
            src_ref=u_out.at[d, sites(c)], dst_ref=u_in.at[d, sites(c)],
            send_sem=bulk_send.at[1, d, c], recv_sem=bulk_recv.at[1, d, c],
            device_id={axis: peer(axis, step)}, device_id_type=MESH)

    def copies(stage, c):
        if stage == 0:
            return [vector_copy(0, d, c, src, halo1) for d in (3, 2, 1, 0)]
        if stage == 1:
            return [product_copy(d, c) for d in (3, 2, 1, 0)]
        return [vector_copy(2, d, c, rounded, halo3) for d in (3, 2, 1, 0)]

    def send(stage, c):
        for copy in copies(stage, c):
            copy.start()

    def send_range(stage, lo, hi):
        @pl.loop(lo, hi)
        def _(c):
            send(stage, c)

    def arrive(stage, c):
        for copy in copies(stage, c):
            copy.wait_recv()

    def scatter(k, off):
        to = peer("ta", off)
        return pltpu.make_async_remote_copy(
            src_ref=packed.at[k, to], dst_ref=parts.at[k, off], send_sem=sum_send.at[k, 0, off],
            recv_sem=sum_recv.at[k, 0, off], device_id={"ta": to}, device_id_type=MESH)

    def spread(k, off):
        return pltpu.make_async_remote_copy(
            src_ref=total.at[k], dst_ref=planes.at[k, me["xy"]], send_sem=sum_send.at[k, 1, off],
            recv_sem=sum_recv.at[k, 1, off], device_id={"xy": peer("xy", off)}, device_id_type=MESH)

    def gather(k, off):
        return pltpu.make_async_remote_copy(
            src_ref=whole.at[k, me["ta"]], dst_ref=whole.at[k, me["ta"]], send_sem=sum_send.at[k, 2, off],
            recv_sem=sum_recv.at[k, 2, off], device_id={"ta": peer("ta", off)}, device_id_type=MESH)

    def came(make, k, off, ref):
        return pltpu.make_async_remote_copy(
            src_ref=ref, dst_ref=ref, send_sem=sum_send.at[k, make, off], recv_sem=sum_recv.at[k, make, off],
            device_id={"ta": peer("ta", 1)}, device_id_type=MESH)

    def sum_start(k, matrix):
        row, col = iotas(half)
        last = matrix[half:, half:]
        mixed = jnp.where(row >= col, matrix[:half, :half], last)
        diag = jnp.sum(jnp.where(row == col, last, 0.0), axis=0, keepdims=True)
        tail = jnp.concatenate([diag, jnp.zeros((1, half), f32)], axis=1)
        tail = jnp.broadcast_to(tail, (n_ta * rows - half, rhs))
        flat = jnp.concatenate([jnp.concatenate([mixed, matrix[half:, :half]], axis=1), tail], axis=0)
        for i in range(n_ta):
            packed[k, i] = flat[i * rows:(i + 1) * rows]
        for off in range(1, n_ta):
            scatter(k, off).start()

    def sum_spread(k):
        value = packed[k, me["ta"]]
        for off in range(1, n_ta):
            came(0, k, off, parts.at[k, off]).wait_recv()
            value = value + parts[k, off]
        total[k] = value
        for off in range(1, n_xy):
            spread(k, off).start()

    def sum_gather(k):
        for off in range(1, n_xy):
            came(1, k, off, planes.at[k, peer("xy", -off)]).wait_recv()
        planes[k, me["xy"]] = total[k]
        value = planes[k, 0]
        for i in range(1, n_xy):
            value = value + planes[k, i]
        whole[k, me["ta"]] = value
        for off in range(1, n_ta):
            gather(k, off).start()

    def sum_done(k):
        for off in range(1, n_ta):
            came(2, k, off, whole.at[k, peer("ta", -off)]).wait_recv()
        flat = jnp.concatenate([whole[k, i] for i in range(n_ta)], axis=0)
        row, col = iotas(half)
        mixed = flat[:half, :half]
        turned = mixed.T
        low = flat[:half, half:]
        first = jnp.where(row >= col, mixed, turned)
        last = jnp.where(row < col, mixed, turned)
        last = jnp.where(row == col, flat[half:half + 1, :half], last)
        return jnp.concatenate([jnp.concatenate([first, low.T], axis=1),
                                jnp.concatenate([low, last], axis=1)], axis=0)

    def sum_waits(k):
        for off in range(1, n_ta):
            scatter(k, off).wait_send()
            gather(k, off).wait_send()
        for off in range(1, n_xy):
            spread(k, off).wait_send()

    def gram(a, b):
        a, b = (v.reshape(-1, rhs) for v in (a, b))
        return mul(a, b, TURNED)

    def near(s):
        y, z = s // nz, lax.rem(s, nz)
        at = lambda i, j: lax.rem(i + ny, ny) * nz + lax.rem(j + nz, nz)
        return at(y + 1, z), at(y - 1, z), at(y, z + 1), at(y, z - 1)

    def apply_near(vector, value, lo, hi):
        @pl.loop(lo, hi)
        def _(s):
            total = mass_term * value(s) + mul(lk[0, s], vector[s], STRAIGHT)
            for k, other in enumerate(near(s)):
                total = total + mul(lk[k + 5, s], vector[other], STRAIGHT)
            acc[s] = total

    def apply_far(s, halo):
        total = acc[s]
        for d in range(4):
            total = total + mul(lk[d + 1, s], halo[d, s], STRAIGHT)
        return total

    def adjoint_near(lo, hi):
        @pl.loop(lo, hi)
        def _(s):
            here = image[s]
            total = mass_term * here.astype(f32) + mul(lk[0, s], here, TURNED)
            plus_y, minus_y, plus_z, minus_z = near(s)
            for k, origin in enumerate((minus_y, plus_y, minus_z, plus_z)):
                total = total + mul(lk[k + 5, origin], image[origin], TURNED).astype(bf16).astype(f32)
            acc[s] = total

    loads = [pltpu.make_async_copy(src, r, local_sem.at[0]), pltpu.make_async_copy(links, lk, local_sem.at[1])]
    for copy in loads:
        copy.start()
    barrier = pltpu.get_barrier_semaphore()
    for axis in ("ta", "xy"):
        for off in range(1, sizes[axis]):
            pl.semaphore_signal(barrier, inc=1, device_id={axis: peer(axis, off)}, device_id_type=MESH)
    pl.semaphore_wait(barrier, n_ta + n_xy - 2)

    def gram_add(high, low):
        gram_ref[...] += gram(high, high)
        cross_ref[...] += gram(low, high)

    def gram_clear():
        gram_ref[...] = jnp.zeros((rhs, rhs), f32)
        cross_ref[...] = jnp.zeros((rhs, rhs), f32)

    def times(high, low, k):
        high, low = high.reshape(-1, rhs), low.reshape(-1, rhs)
        out = mul(high, coef[2 * k], STRAIGHT) + mul(high, coef[2 * k + 1], STRAIGHT) + mul(low, coef[2 * k], STRAIGHT)
        return out.reshape(per, comp, rhs)

    def source_times(c, k):
        high = r[sites(c)].reshape(-1, rhs)
        return (mul(high, coef[2 * k], STRAIGHT) + mul(high, coef[2 * k + 1], STRAIGHT)).reshape(per, comp, rhs)

    def keep(k, value):
        high, low = split(value)
        coef[2 * k] = high
        coef[2 * k + 1] = low

    send_range(0, 0, EARLY[0])
    loads[0].wait()
    sum_start(0, gram(r[...], r[...]))
    loads[1].wait()
    apply_near(r, lambda s: r[s].astype(f32), 0, per * 2)
    sum_spread(0)
    send_range(0, EARLY[0], CHUNKS)
    apply_near(r, lambda s: r[s].astype(f32), per * 2, n)
    gram_clear()
    sum_gather(0)
    sums[0] = sum_done(0)
    eliminated(sums[0], work)
    inverse0[...] = work[0]

    def first(c):
        arrive(0, c)

        @pl.loop(0, per)
        def _(j):
            s = c * per + j
            value = apply_far(s, halo1)
            here, low = split(value)
            full[s] = value
            image[s] = here
            rounded[s] = low
            for d in range(4):
                u_out[d, s] = mul(lk[d + 1, s], here, TURNED).astype(bf16)

        gram_add(image[sites(c)], rounded[sites(c)])

    @pl.loop(0, EARLY[1])
    def _(c):
        first(c)
        send(1, c)

    @pl.loop(EARLY[1], CHUNKS)
    def _(c):
        first(c)

    sum_start(1, gram_ref[...] + 0.5 * (cross_ref[...] + cross_ref[...].T))
    adjoint_near(0, per * 2)
    sum_spread(1)
    send_range(1, EARLY[1], CHUNKS)
    adjoint_near(per * 2, n)
    gram_clear()

    def second(c):
        arrive(1, c)

        @pl.loop(0, per)
        def _(j):
            s = c * per + j
            value = acc[s]
            for d in range(4):
                value = value + u_in[d, s].astype(f32)
            normal[s] = value
            rounded[s] = value.astype(bf16)

    @pl.loop(0, EARLY[2])
    def _(c):
        second(c)
        send(2, c)

    sum_gather(1)
    sums[1] = sum_done(1)
    eliminated(sums[1], work)
    keep(0, solved(sums[1], work[0], sums[0]))

    @pl.loop(EARLY[2], CHUNKS)
    def _(c):
        second(c)

    @pl.loop(0, CHUNKS)
    def _(c):
        value, high = normal[sites(c)], rounded[sites(c)]
        here = r[sites(c)].astype(f32) - times(high, (value - high.astype(f32)).astype(bf16), 0)
        residual[sites(c)] = here
        gram_add(*split(here))

    sum_start(2, gram_ref[...] + cross_ref[...] + cross_ref[...].T)
    apply_near(rounded, lambda s: normal[s], 0, per * 2)
    sum_spread(2)
    send_range(2, EARLY[2], CHUNKS)
    apply_near(rounded, lambda s: normal[s], per * 2, n)
    gram_clear()
    for c in range(CHUNKS):
        for copy in copies(1, c):
            copy.wait_send()
    sum_gather(2)
    fresh_ref[...] = sum_done(2)
    beta = solved(sums[0], inverse0[...], fresh_ref[...])
    keep(1, beta)
    curvature_ref[...] = dot_t(beta, dot(sums[1], beta))

    @pl.loop(0, CHUNKS)
    def _(c):
        normal[sites(c)] = source_times(c, 0)
        high, low = split(residual[sites(c)] + source_times(c, 1))
        u_out[0, sites(c)] = high
        u_out[1, sites(c)] = low

    outs = [pltpu.make_async_copy(source, target, local_sem.at[2 + k]) for k, (source, target) in enumerate(
        ((normal, first_ref), (u_out.at[0], high_ref), (u_out.at[1], low_ref)))]
    for copy in outs:
        copy.start()

    @pl.loop(0, CHUNKS)
    def _(c):
        arrive(2, c)

        @pl.loop(0, per)
        def _(j):
            s = c * per + j
            acc[s] = apply_far(s, halo3)

        here = (full[sites(c)] - times(*split(acc[sites(c)]), 0)).astype(bf16)
        gram_ref[...] += gram(here, here)

    sum_start(3, gram_ref[...])
    sum_spread(3)
    sum_gather(3)
    for copy in outs:
        copy.wait()
    for stage in (0, 2):
        @pl.loop(0, CHUNKS)
        def _(c):
            for copy in copies(stage, c):
                copy.wait_send()
    curvature = sum_done(3) - curvature_ref[...]
    curvature_ref[...] = 0.5 * (curvature + curvature.T)
    for k in range(SUMS):
        sum_waits(k)


def krylov(sources, links, sizes):
    ny, nt, nx, nz, comp, rhs = sources.shape
    assert nt == 1 and nx == 1
    n = ny * nz
    n_ta, n_xy = sizes["ta"], sizes["xy"]
    rows = piece_rows(rhs, n_ta)
    anywhere = pl.BlockSpec(memory_space=pl.ANY)
    vmem = pl.BlockSpec(memory_space=pltpu.VMEM)
    slab = lambda *lead: pltpu.VMEM(lead + (n, comp, rhs), bf16)
    wide = pltpu.VMEM((n, comp, rhs), f32)
    pieces = lambda count: pltpu.VMEM((SUMS, count, rows, rhs), f32)
    most = max(n_ta, n_xy)
    square = lambda *lead: pltpu.VMEM(lead + (rhs, rhs), f32)
    return pl.pallas_call(
        functools.partial(krylov_kernel, sizes, ny, nz),
        out_shape=[jax.ShapeDtypeStruct((n, comp, rhs), d) for d in (f32, bf16, bf16)]
        + [jax.ShapeDtypeStruct((rhs, rhs), f32)] * 2,
        in_specs=[anywhere, anywhere],
        out_specs=[anywhere] * 3 + [vmem] * 2,
        scratch_shapes=[
            slab(), pltpu.VMEM((links.shape[0], n, comp, comp), bf16), slab(4), slab(4), slab(4), slab(4), slab(), slab(),
            wide, wide, wide, wide, square(), square(), square(2), square(), square(2), pltpu.VMEM((4, rhs, rhs), bf16),
            pieces(n_ta), pieces(n_ta), pltpu.VMEM((SUMS, rows, rhs), f32), pieces(n_xy), pieces(n_ta),
            pltpu.SemaphoreType.DMA((5,)), pltpu.SemaphoreType.DMA((3, 4, CHUNKS)), pltpu.SemaphoreType.DMA((3, 4, CHUNKS)),
            pltpu.SemaphoreType.DMA((SUMS, 3, most)), pltpu.SemaphoreType.DMA((SUMS, 3, most)),
        ],
        cost_estimate=pl.CostEstimate(flops=int(6e9), bytes_accessed=64 << 20, transcendentals=0),
        compiler_params=pltpu.CompilerParams(collective_id=0, has_side_effects=True, vmem_limit_bytes=67043328),
    )(sources.reshape(n, comp, rhs), links.reshape(links.shape[0], n, comp, comp))


dot = functools.partial(jnp.dot, precision=HI, preferred_element_type=f32)


def dot_t(a, b):
    return lax.dot_general(a, b, TURNED, precision=HI, preferred_element_type=f32)


def split(value):
    high = value.astype(bf16)
    return high, (value - high.astype(f32)).astype(bf16)


def scaled(a):
    row, col = iotas(a.shape[0])
    eye = jnp.where(row == col, 1.0, 0.0).astype(f32)
    diag = a * eye
    down = lax.rsqrt(jnp.sum(diag, axis=1, keepdims=True))
    across = lax.rsqrt(jnp.sum(diag, axis=0, keepdims=True))
    return a * down * across, eye, down, across


def eliminate(x_ref, n):
    row, col = iotas(n)

    def step(k, carry):
        m = x_ref[...]
        pivot_row = x_ref[pl.ds(k, 1), :]
        here = col == k
        pivot_col = jnp.sum(jnp.where(here, m, 0.0), axis=1, keepdims=True)
        hit = here[:1]
        inv = 1.0 / jnp.sum(jnp.where(hit, pivot_row, 0.0), axis=1, keepdims=True)
        line = jnp.where(hit, inv, pivot_row * inv)
        m = jnp.where(here, 0.0, m) - pivot_col * line
        x_ref[...] = jnp.where(row == k, line, m)
        return carry

    lax.fori_loop(0, n, step, 0)


def refined(a, x, eye, down, across):
    x = x + dot(x, eye - dot(a, x))
    return x * down * across


def eliminated(a, work):
    a, eye, down, across = scaled(a)
    work[0] = a
    work[1] = a
    eliminate(work.at[0], a.shape[0])
    work[0] = refined(work[1], work[0], eye, down, across)


def invert(a, x_ref, s_ref, p_ref):
    a, eye, down, across = scaled(a)
    s_ref[...] = a
    p_ref[...] = eye - a
    x_ref[...] = eye + p_ref[...]

    def square(_, carry):
        power = dot(p_ref[...], p_ref[...])
        p_ref[...] = power
        x_ref[...] = x_ref[...] + dot(x_ref[...], power)
        return carry

    lax.fori_loop(0, 3, square, 0)
    worst = jnp.max(jnp.abs(eye - dot(a, x_ref[...])))

    @pl.when(jnp.logical_not(worst < 1e-3))
    def _():
        x_ref[...] = s_ref[...]
        eliminate(x_ref, a.shape[0])

    return refined(s_ref[...], x_ref[...], eye, down, across)


def solved(a, inverse, right):
    out = dot(inverse, right)
    return out + dot(inverse, right - dot(a, out))


def closing_kernel(chunks, curvature_ref, fresh_ref, first_hbm, high_hbm, low_hbm, out_hbm,
                   first, high, low, coef, x_ref, s_ref, p_ref, load_sem, store_sem):
    n, comp, rhs = first.shape
    per = n // chunks
    loads = [pltpu.make_async_copy(source, target, load_sem.at[k]) for k, (source, target) in enumerate(
        ((first_hbm, first), (high_hbm, high), (low_hbm, low)))]
    for copy in loads:
        copy.start()
    curvature, fresh = curvature_ref[...], fresh_ref[...]
    alpha = solved(curvature, invert(curvature, x_ref, s_ref, p_ref), fresh)
    coef[0], coef[1] = split(alpha)
    for copy in loads:
        copy.wait()

    def store(c):
        return pltpu.make_async_copy(first.at[pl.ds(c * per, per)], out_hbm.at[pl.ds(c * per, per)], store_sem.at[c])

    @pl.loop(0, chunks)
    def _(c):
        here = pl.ds(c * per, per)
        left, rest = high[here].reshape(-1, rhs), low[here].reshape(-1, rhs)
        step = mul(left, coef[0], STRAIGHT) + mul(left, coef[1], STRAIGHT) + mul(rest, coef[0], STRAIGHT)
        first[here] = first[here] + step.reshape(per, comp, rhs)
        store(c).start()

    @pl.loop(0, chunks)
    def _(c):
        store(c).wait()


def closing(first, high, low, curvature, fresh):
    vmem, anywhere = pl.BlockSpec(memory_space=pltpu.VMEM), pl.BlockSpec(memory_space=pl.ANY)
    rhs = fresh.shape[0]
    return pl.pallas_call(
        functools.partial(closing_kernel, CHUNKS),
        out_shape=jax.ShapeDtypeStruct(first.shape, f32),
        in_specs=[vmem] * 2 + [anywhere] * 3,
        out_specs=anywhere,
        scratch_shapes=[pltpu.VMEM(first.shape, f32), pltpu.VMEM(first.shape, bf16), pltpu.VMEM(first.shape, bf16),
                        pltpu.VMEM((2, rhs, rhs), bf16)] + [pltpu.VMEM((rhs, rhs), f32)] * 3
        + [pltpu.SemaphoreType.DMA((3,)), pltpu.SemaphoreType.DMA((CHUNKS,))],
        cost_estimate=pl.CostEstimate(flops=int(4e9), bytes_accessed=10 << 20, transcendentals=0),
    )(curvature, fresh, first, high, low)


def solution(mesh):
    sizes = {axis: mesh.shape[axis] for axis in ("ta", "xy")}

    def body(sources, links):
        return closing(*krylov(sources, links, sizes)).reshape(sources.shape)

    return jax.shard_map(
        body,
        mesh=mesh,
        in_specs=(
            P("groups", "ta", "xy", None, None, None),
            P("groups", None, "ta", "xy", None, None, None),
        ),
        out_specs=P("groups", "ta", "xy", None, None, None),
        check_vma=False,
    )
```

profile of v0, /device:TPU:0, one launch (start us, length us, event | category | flops | bytes accessed | tf_op | source)
XLA Modules:
  0.0 300.9 jit_solution(12398996082776954215)
XLA Ops:
  0.0 255.7 %shard_map.28 = (f32[32,96,256]{2,1,0:T(8,128)}, bf16[32,96,256]{2,1,0:T(8,128)(2,1)}, bf16[32,96,256]{2,1,0:T(8,128)(2,1)}, f32[256,256]{1,0:T(8,128)}, f32[256,256]{1,0:T(8,128)}) custom-call(bf16[32,96,256]{2,1,0:T(8,128)(2,1)} %bitcast.6, bf16[9,32,96,96]{3,2,1,0:T(8,128)(2,1)} %bitcast.5), custom_call_target="tpu_custom_call" | custom-call | flops 6000000000 | bytes 67108864 | tf_op jit(solution)/shard_map/pallas_call | solution.py:370
  255.7 45.2 %shard_map.29 = f32[32,96,256]{2,1,0:T(8,128)} custom-call(f32[256,256]{1,0:T(8,128)} %get-tuple-element.10.curvature_ref, f32[256,256]{1,0:T(8,128)} %get-tuple-element.11.fresh_ref, f32[32,96,256]{2,1,0:T(8,128)} %get-tuple-element.12.first_hbm, bf16[32,96,256]{2,1,0:T(8,128)(2,1)} %get-tuple-element.13.high_hbm, ...), custom_call_target="tpu_custom_call" | custom-call | flops 4000000000 | bytes 10485760 | tf_op jit(solution)/shard_map/pallas_call | solution.py:501
where the time goes:
time: 301 us
  Pallas kernels  301 us (100%)
    pallas_call x1, Pallas kernels, krylov(): pl.pallas_call(functools.partial(krylov_kernel, sizes, ny, nz), out_shape...  256 us
    pallas_call x1, Pallas kernels, closing(): pl.pallas_call(functools.partial(closing_kernel, CHUNKS), out_shape=jax.S...  45.2 us

commit v1 on v0

--- a/solution.py
+++ b/solution.py
@@ -15,7 +15,7 @@
 
 HOPS = (("ta", 1), ("ta", -1), ("xy", 1), ("xy", -1))
 CHUNKS = 8
-EARLY = (2, 2, 3)
+EARLY = (2, 1, 2)
 SUMS = 4
 
 mul = functools.partial(lax.dot_general, preferred_element_type=f32)
@@ -28,7 +28,7 @@
 
 
 def piece_rows(rhs, n_ta):
-    return -(-(rhs // 2 + 8) // (8 * n_ta)) * 8
+    return -(-(rhs + 1) // (8 * n_ta)) * 8
 
 
 def krylov_kernel(sizes, ny, nz, src, links, first_ref, high_ref, low_ref, curvature_ref, fresh_ref,
@@ -107,9 +107,8 @@
         last = matrix[half:, half:]
         mixed = jnp.where(row >= col, matrix[:half, :half], last)
         diag = jnp.sum(jnp.where(row == col, last, 0.0), axis=0, keepdims=True)
-        tail = jnp.concatenate([diag, jnp.zeros((1, half), f32)], axis=1)
-        tail = jnp.broadcast_to(tail, (n_ta * rows - half, rhs))
-        flat = jnp.concatenate([jnp.concatenate([mixed, matrix[half:, :half]], axis=1), tail], axis=0)
+        tail = jnp.broadcast_to(diag, (n_ta * rows - rhs, half))
+        flat = jnp.concatenate([mixed, matrix[half:, :half], tail], axis=0)
         for i in range(n_ta):
             packed[k, i] = flat[i * rows:(i + 1) * rows]
         for off in range(1, n_ta):
@@ -140,12 +139,11 @@
             came(2, k, off, whole.at[k, peer("ta", -off)]).wait_recv()
         flat = jnp.concatenate([whole[k, i] for i in range(n_ta)], axis=0)
         row, col = iotas(half)
-        mixed = flat[:half, :half]
+        mixed, low = flat[:half], flat[half:rhs]
         turned = mixed.T
-        low = flat[:half, half:]
         first = jnp.where(row >= col, mixed, turned)
         last = jnp.where(row < col, mixed, turned)
-        last = jnp.where(row == col, flat[half:half + 1, :half], last)
+        last = jnp.where(row == col, flat[rhs:rhs + 1], last)
         return jnp.concatenate([jnp.concatenate([first, low.T], axis=1),
                                 jnp.concatenate([low, last], axis=1)], axis=0)
 
@@ -220,6 +218,9 @@
         coef[2 * k] = high
         coef[2 * k + 1] = low
 
+    def share(i, count, whole=rhs):
+        return whole * i // count, whole * (i + 1) // count
+
     send_range(0, 0, EARLY[0])
     loads[0].wait()
     sum_start(0, gram(r[...], r[...]))
@@ -229,11 +230,6 @@
     send_range(0, EARLY[0], CHUNKS)
     apply_near(r, lambda s: r[s].astype(f32), per * 2, n)
     gram_clear()
-    sum_gather(0)
-    sums[0] = sum_done(0)
-    eliminated(sums[0], work)
-    inverse0[...] = work[0]
-
     def first(c):
         arrive(0, c)
 
@@ -250,14 +246,17 @@
 
         gram_add(image[sites(c)], rounded[sites(c)])
 
-    @pl.loop(0, EARLY[1])
-    def _(c):
+    for c in range(CHUNKS):
         first(c)
-        send(1, c)
-
-    @pl.loop(EARLY[1], CHUNKS)
-    def _(c):
-        first(c)
+        if c < EARLY[1]:
+            send(1, c)
+        if c == EARLY[0] - 1:
+            sum_gather(0)
+        if c == EARLY[0]:
+            sums[0] = sum_done(0)
+            elimination_begin(sums[0], work)
+        if EARLY[0] <= c < CHUNKS - 1:
+            eliminate(work.at[0], *share(c - EARLY[0], CHUNKS - EARLY[0]))
 
     sum_start(1, gram_ref[...] + 0.5 * (cross_ref[...] + cross_ref[...].T))
     adjoint_near(0, per * 2)
@@ -265,6 +264,8 @@
     send_range(1, EARLY[1], CHUNKS)
     adjoint_near(per * 2, n)
     gram_clear()
+    eliminate(work.at[0], share(CHUNKS - 1 - EARLY[0], CHUNKS - EARLY[0])[0], rhs)
+    inverse0[...] = elimination_end(sums[0], work)
 
     def second(c):
         arrive(1, c)
@@ -278,26 +279,32 @@
             normal[s] = value
             rounded[s] = value.astype(bf16)
 
-    @pl.loop(0, EARLY[2])
-    def _(c):
-        second(c)
-        send(2, c)
-
-    sum_gather(1)
-    sums[1] = sum_done(1)
-    eliminated(sums[1], work)
-    keep(0, solved(sums[1], work[0], sums[0]))
-
-    @pl.loop(EARLY[2], CHUNKS)
-    def _(c):
-        second(c)
-
-    @pl.loop(0, CHUNKS)
-    def _(c):
+    def third(c):
         value, high = normal[sites(c)], rounded[sites(c)]
         here = r[sites(c)].astype(f32) - times(high, (value - high.astype(f32)).astype(bf16), 0)
         residual[sites(c)] = here
         gram_add(*split(here))
+
+    ahead = CHUNKS - 2
+    for c in range(ahead):
+        second(c)
+        if c < EARLY[2]:
+            send(2, c)
+        if c == 0:
+            sum_gather(1)
+            sums[1] = sum_done(1)
+            elimination_begin(sums[1], work)
+        eliminate(work.at[0], *share(c, ahead))
+    keep(0, solved(sums[1], elimination_end(sums[1], work), sums[0]))
+
+    @pl.loop(0, ahead)
+    def _(c):
+        third(c)
+
+    @pl.loop(ahead, CHUNKS)
+    def _(c):
+        second(c)
+        third(c)
 
     sum_start(2, gram_ref[...] + cross_ref[...] + cross_ref[...].T)
     apply_near(rounded, lambda s: normal[s], 0, per * 2)
@@ -305,17 +312,23 @@
     send_range(2, EARLY[2], CHUNKS)
     apply_near(rounded, lambda s: normal[s], per * 2, n)
     gram_clear()
-    for c in range(CHUNKS):
+    @pl.loop(0, CHUNKS)
+    def _(c):
         for copy in copies(1, c):
             copy.wait_send()
-    sum_gather(2)
-    fresh_ref[...] = sum_done(2)
-    beta = solved(sums[0], inverse0[...], fresh_ref[...])
-    keep(1, beta)
-    curvature_ref[...] = dot_t(beta, dot(sums[1], beta))
-
-    @pl.loop(0, CHUNKS)
-    def _(c):
+
+    def fourth(c):
+        arrive(2, c)
+
+        @pl.loop(0, per)
+        def _(j):
+            s = c * per + j
+            acc[s] = apply_far(s, halo3)
+
+        here = (full[sites(c)] - times(*split(acc[sites(c)]), 0)).astype(bf16)
+        gram_ref[...] += gram(here, here)
+
+    def fifth(c):
         normal[sites(c)] = source_times(c, 0)
         high, low = split(residual[sites(c)] + source_times(c, 1))
         u_out[0, sites(c)] = high
@@ -323,20 +336,22 @@
 
     outs = [pltpu.make_async_copy(source, target, local_sem.at[2 + k]) for k, (source, target) in enumerate(
         ((normal, first_ref), (u_out.at[0], high_ref), (u_out.at[1], low_ref)))]
-    for copy in outs:
-        copy.start()
-
-    @pl.loop(0, CHUNKS)
-    def _(c):
-        arrive(2, c)
-
-        @pl.loop(0, per)
-        def _(j):
-            s = c * per + j
-            acc[s] = apply_far(s, halo3)
-
-        here = (full[sites(c)] - times(*split(acc[sites(c)]), 0)).astype(bf16)
-        gram_ref[...] += gram(here, here)
+    begin = EARLY[2] + 1
+    for c in range(CHUNKS):
+        fourth(c)
+        if c == EARLY[2] - 1:
+            sum_gather(2)
+        if c == EARLY[2]:
+            fresh_ref[...] = sum_done(2)
+            beta = solved(sums[0], inverse0[...], fresh_ref[...])
+            keep(1, beta)
+            curvature_ref[...] = dot_t(beta, dot(sums[1], beta))
+        if begin <= c < CHUNKS - 1:
+            lo, hi = share(c - begin, CHUNKS - 1 - begin, CHUNKS)
+            pl.loop(lo, hi)(fifth)
+        if c == CHUNKS - 2:
+            for copy in outs:
+                copy.start()
 
     sum_start(3, gram_ref[...])
     sum_spread(3)
@@ -364,7 +379,7 @@
     vmem = pl.BlockSpec(memory_space=pltpu.VMEM)
     slab = lambda *lead: pltpu.VMEM(lead + (n, comp, rhs), bf16)
     wide = pltpu.VMEM((n, comp, rhs), f32)
-    pieces = lambda count: pltpu.VMEM((SUMS, count, rows, rhs), f32)
+    pieces = lambda count: pltpu.VMEM((SUMS, count, rows, rhs // 2), f32)
     most = max(n_ta, n_xy)
     square = lambda *lead: pltpu.VMEM(lead + (rhs, rhs), f32)
     return pl.pallas_call(
@@ -376,7 +391,7 @@
         scratch_shapes=[
             slab(), pltpu.VMEM((links.shape[0], n, comp, comp), bf16), slab(4), slab(4), slab(4), slab(4), slab(), slab(),
             wide, wide, wide, wide, square(), square(), square(2), square(), square(2), pltpu.VMEM((4, rhs, rhs), bf16),
-            pieces(n_ta), pieces(n_ta), pltpu.VMEM((SUMS, rows, rhs), f32), pieces(n_xy), pieces(n_ta),
+            pieces(n_ta), pieces(n_ta), pltpu.VMEM((SUMS, rows, rhs // 2), f32), pieces(n_xy), pieces(n_ta),
             pltpu.SemaphoreType.DMA((5,)), pltpu.SemaphoreType.DMA((3, 4, CHUNKS)), pltpu.SemaphoreType.DMA((3, 4, CHUNKS)),
             pltpu.SemaphoreType.DMA((SUMS, 3, most)), pltpu.SemaphoreType.DMA((SUMS, 3, most)),
         ],
@@ -406,8 +421,8 @@
     return a * down * across, eye, down, across
 
 
-def eliminate(x_ref, n):
-    row, col = iotas(n)
+def eliminate(x_ref, lo, hi):
+    row, col = iotas(x_ref.shape[0])
 
     def step(k, carry):
         m = x_ref[...]
@@ -421,7 +436,16 @@
         x_ref[...] = jnp.where(row == k, line, m)
         return carry
 
-    lax.fori_loop(0, n, step, 0)
+    lax.fori_loop(lo, hi, step, 0)
+
+
+def elimination_begin(a, work):
+    work[0] = work[1] = scaled(a)[0]
+
+
+def elimination_end(a, work):
+    _, eye, down, across = scaled(a)
+    return refined(work[1], work[0], eye, down, across)
 
 
 def refined(a, x, eye, down, across):
@@ -429,53 +453,47 @@
     return x * down * across
 
 
-def eliminated(a, work):
-    a, eye, down, across = scaled(a)
-    work[0] = a
-    work[1] = a
-    eliminate(work.at[0], a.shape[0])
-    work[0] = refined(work[1], work[0], eye, down, across)
-
-
-def invert(a, x_ref, s_ref, p_ref):
-    a, eye, down, across = scaled(a)
-    s_ref[...] = a
-    p_ref[...] = eye - a
-    x_ref[...] = eye + p_ref[...]
-
-    def square(_, carry):
-        power = dot(p_ref[...], p_ref[...])
-        p_ref[...] = power
-        x_ref[...] = x_ref[...] + dot(x_ref[...], power)
-        return carry
-
-    lax.fori_loop(0, 3, square, 0)
-    worst = jnp.max(jnp.abs(eye - dot(a, x_ref[...])))
-
-    @pl.when(jnp.logical_not(worst < 1e-3))
-    def _():
-        x_ref[...] = s_ref[...]
-        eliminate(x_ref, a.shape[0])
-
-    return refined(s_ref[...], x_ref[...], eye, down, across)
-
-
 def solved(a, inverse, right):
     out = dot(inverse, right)
     return out + dot(inverse, right - dot(a, out))
 
 
+def solve(a, right, x_ref, s_ref, out_ref):
+    s, eye, down, across = scaled(a)
+    power = eye - s
+    near = power.astype(bf16)
+    square = mul(near, near, STRAIGHT)
+    near2 = square.astype(bf16)
+    fourth = mul(near2, near2, STRAIGHT).astype(bf16)
+    inverse = eye + power + square + mul(near, near2, STRAIGHT)
+    inverse = (inverse + mul(inverse.astype(bf16), fourth, STRAIGHT)).astype(bf16)
+    off = jnp.abs(eye - mul(s.astype(bf16), inverse, STRAIGHT))
+    worst = jnp.max(jnp.sum(off, axis=1, keepdims=True))
+    right = right * down
+    x = mul(inverse, right.astype(bf16), STRAIGHT)
+    for _ in range(2):
+        x = x + mul(inverse, (right - dot(s, x)).astype(bf16), STRAIGHT)
+    out_ref[...] = x * down
+
+    @pl.when(jnp.logical_not(worst < 0.05))
+    def _():
+        s_ref[...] = s
+        x_ref[...] = s
+        eliminate(x_ref, 0, a.shape[0])
+        x = refined(s_ref[...], x_ref[...], eye, 1.0, 1.0)
+        out_ref[...] = solved(s_ref[...], x, right) * down
+
+
 def closing_kernel(chunks, curvature_ref, fresh_ref, first_hbm, high_hbm, low_hbm, out_hbm,
-                   first, high, low, coef, x_ref, s_ref, p_ref, load_sem, store_sem):
+                   first, high, low, coef, x_ref, s_ref, alpha_ref, load_sem, store_sem):
     n, comp, rhs = first.shape
     per = n // chunks
     loads = [pltpu.make_async_copy(source, target, load_sem.at[k]) for k, (source, target) in enumerate(
         ((first_hbm, first), (high_hbm, high), (low_hbm, low)))]
     for copy in loads:
         copy.start()
-    curvature, fresh = curvature_ref[...], fresh_ref[...]
-    alpha = solved(curvature, invert(curvature, x_ref, s_ref, p_ref), fresh)
-    coef[0], coef[1] = split(alpha)
+    solve(curvature_ref[...], fresh_ref[...], x_ref, s_ref, alpha_ref)
+    coef[0], coef[1] = split(alpha_ref[...])
     for copy in loads:
         copy.wait()
 

time: 301 us -> 293 us (0.973)
  Pallas kernels: 301 us -> 293 us
    pallas_call x1, Pallas kernels: 256 us -> 250 us  [krylov(): pl.pallas_call(functools.partial(krylov_kernel, sizes, ny, nz), out_shape...]
where the time goes in v1:
time: 293 us
  Pallas kernels  293 us (100%)
    pallas_call x1, Pallas kernels, krylov(): pl.pallas_call(functools.partial(krylov_kernel, sizes, ny, nz), out_shape...  250 us
    pallas_call x1, Pallas kernels, closing(): pl.pallas_call(functools.partial(closing_kernel, CHUNKS), out_shape=jax.S...  43.2 us

profile of v1, /device:TPU:0, one launch (start us, length us, event | category | flops | bytes accessed | tf_op | source)
XLA Modules:
  0.0 293.0 jit_solution(8254062475982604299)
XLA Ops:
  0.0 249.6 %shard_map.28 = (f32[32,96,256]{2,1,0:T(8,128)}, bf16[32,96,256]{2,1,0:T(8,128)(2,1)}, bf16[32,96,256]{2,1,0:T(8,128)(2,1)}, f32[256,256]{1,0:T(8,128)}, f32[256,256]{1,0:T(8,128)}) custom-call(bf16[32,96,256]{2,1,0:T(8,128)(2,1)} %bitcast.6, bf16[9,32,96,96]{3,2,1,0:T(8,128)(2,1)} %bitcast.5), custom_call_target="tpu_custom_call" | custom-call | flops 6000000000 | bytes 67108864 | tf_op jit(solution)/shard_map/pallas_call | solution.py:385
  249.6 43.2 %shard_map.29 = f32[32,96,256]{2,1,0:T(8,128)} custom-call(f32[256,256]{1,0:T(8,128)} %get-tuple-element.10.curvature_ref, f32[256,256]{1,0:T(8,128)} %get-tuple-element.11.fresh_ref, f32[32,96,256]{2,1,0:T(8,128)} %get-tuple-element.12.first_hbm, bf16[32,96,256]{2,1,0:T(8,128)(2,1)} %get-tuple-element.13.high_hbm, ...), custom_call_target="tpu_custom_call" | custom-call | flops 4000000000 | bytes 10485760 | tf_op jit(solution)/shard_map/pallas_call | solution.py:519

commit v2 on v1

--- a/solution.py
+++ b/solution.py
@@ -15,7 +15,7 @@
 
 HOPS = (("ta", 1), ("ta", -1), ("xy", 1), ("xy", -1))
 CHUNKS = 8
-EARLY = (2, 1, 2)
+EARLY = (2, 3, 4)
 SUMS = 4
 
 mul = functools.partial(lax.dot_general, preferred_element_type=f32)

time: 293 us -> 278 us (0.949)
  Pallas kernels: 293 us -> 278 us
    pallas_call x1, Pallas kernels: 250 us -> 234 us  [krylov(): pl.pallas_call(functools.partial(krylov_kernel, sizes, ny, nz), out_shape...]
where the time goes in v2:
time: 278 us
  Pallas kernels  278 us (100%)
    pallas_call x1, Pallas kernels, krylov(): pl.pallas_call(functools.partial(krylov_kernel, sizes, ny, nz), out_shape...  234 us
    pallas_call x1, Pallas kernels, closing(): pl.pallas_call(functools.partial(closing_kernel, CHUNKS), out_shape=jax.S...  43.2 us

profile of v2, /device:TPU:0, one launch (start us, length us, event | category | flops | bytes accessed | tf_op | source)
XLA Modules:
  0.0 277.8 jit_solution(10886529774566305545)
XLA Ops:
  0.0 234.4 %shard_map.28 = (f32[32,96,256]{2,1,0:T(8,128)}, bf16[32,96,256]{2,1,0:T(8,128)(2,1)}, bf16[32,96,256]{2,1,0:T(8,128)(2,1)}, f32[256,256]{1,0:T(8,128)}, f32[256,256]{1,0:T(8,128)}) custom-call(bf16[32,96,256]{2,1,0:T(8,128)(2,1)} %bitcast.6, bf16[9,32,96,96]{3,2,1,0:T(8,128)(2,1)} %bitcast.5), custom_call_target="tpu_custom_call" | custom-call | flops 6000000000 | bytes 67108864 | tf_op jit(solution)/shard_map/pallas_call | solution.py:385
  234.4 43.2 %shard_map.29 = f32[32,96,256]{2,1,0:T(8,128)} custom-call(f32[256,256]{1,0:T(8,128)} %get-tuple-element.10.curvature_ref, f32[256,256]{1,0:T(8,128)} %get-tuple-element.11.fresh_ref, f32[32,96,256]{2,1,0:T(8,128)} %get-tuple-element.12.first_hbm, bf16[32,96,256]{2,1,0:T(8,128)(2,1)} %get-tuple-element.13.high_hbm, ...), custom_call_target="tpu_custom_call" | custom-call | flops 4000000000 | bytes 10485760 | tf_op jit(solution)/shard_map/pallas_call | solution.py:519

commit v3 on v2

--- a/solution.py
+++ b/solution.py
@@ -17,6 +17,7 @@
 CHUNKS = 8
 EARLY = (2, 3, 4)
 SUMS = 4
+PARTS = 3
 
 mul = functools.partial(lax.dot_general, preferred_element_type=f32)
 STRAIGHT = (((1,), (0,)), ((), ()))
@@ -31,8 +32,8 @@
     return -(-(rhs + 1) // (8 * n_ta)) * 8
 
 
-def krylov_kernel(sizes, ny, nz, src, links, first_ref, high_ref, low_ref, curvature_ref, fresh_ref,
-                  r, lk, halo1, halo3, u_out, u_in, image, rounded, acc, full, normal, residual, gram_ref, cross_ref, work, inverse0,
+def krylov_kernel(sizes, ny, nz, src, links, first_ref, second_ref, high_ref, low_ref, curvature_ref, fresh_ref,
+                  r, lk, halo, u_out, u_in, image, rounded, acc, full, normal, gram_ref, cross_ref, work, inverse0,
                   sums, coef, packed, parts, total, planes, whole, local_sem, bulk_send, bulk_recv, sum_send, sum_recv):
     n_ta, n_xy = sizes["ta"], sizes["xy"]
     me = {axis: lax.axis_index(axis) for axis in sizes}
@@ -63,10 +64,10 @@
 
     def copies(stage, c):
         if stage == 0:
-            return [vector_copy(0, d, c, src, halo1) for d in (3, 2, 1, 0)]
+            return [vector_copy(0, d, c, src, halo) for d in (3, 2, 1, 0)]
         if stage == 1:
             return [product_copy(d, c) for d in (3, 2, 1, 0)]
-        return [vector_copy(2, d, c, rounded, halo3) for d in (3, 2, 1, 0)]
+        return [vector_copy(2, d, c, rounded, halo) for d in (3, 2, 1, 0)]
 
     def send(stage, c):
         for copy in copies(stage, c):
@@ -81,26 +82,25 @@
         for copy in copies(stage, c):
             copy.wait_recv()
 
-    def scatter(k, off):
-        to = peer("ta", off)
+    tiles = rows // 8
+    parts_of = [pl.ds(8 * (tiles * p // PARTS), 8 * (tiles * (p + 1) // PARTS - tiles * p // PARTS)) for p in range(PARTS)]
+
+    def sum_copy(k, stage, p, off, axis, source, target):
         return pltpu.make_async_remote_copy(
-            src_ref=packed.at[k, to], dst_ref=parts.at[k, off], send_sem=sum_send.at[k, 0, off],
-            recv_sem=sum_recv.at[k, 0, off], device_id={"ta": to}, device_id_type=MESH)
-
-    def spread(k, off):
-        return pltpu.make_async_remote_copy(
-            src_ref=total.at[k], dst_ref=planes.at[k, me["xy"]], send_sem=sum_send.at[k, 1, off],
-            recv_sem=sum_recv.at[k, 1, off], device_id={"xy": peer("xy", off)}, device_id_type=MESH)
-
-    def gather(k, off):
-        return pltpu.make_async_remote_copy(
-            src_ref=whole.at[k, me["ta"]], dst_ref=whole.at[k, me["ta"]], send_sem=sum_send.at[k, 2, off],
-            recv_sem=sum_recv.at[k, 2, off], device_id={"ta": peer("ta", off)}, device_id_type=MESH)
-
-    def came(make, k, off, ref):
-        return pltpu.make_async_remote_copy(
-            src_ref=ref, dst_ref=ref, send_sem=sum_send.at[k, make, off], recv_sem=sum_recv.at[k, make, off],
-            device_id={"ta": peer("ta", 1)}, device_id_type=MESH)
+            src_ref=source.at[parts_of[p]], dst_ref=target.at[parts_of[p]], send_sem=sum_send.at[k, stage, p, off],
+            recv_sem=sum_recv.at[k, stage, p, off], device_id={axis: peer(axis, off)}, device_id_type=MESH)
+
+    def scatter(k, p, off):
+        return sum_copy(k, 0, p, off, "ta", packed.at[k, peer("ta", off)], parts.at[k, off])
+
+    def spread(k, p, off):
+        return sum_copy(k, 1, p, off, "xy", total.at[k], planes.at[k, me["xy"]])
+
+    def gather(k, p, off):
+        return sum_copy(k, 2, p, off, "ta", whole.at[k, me["ta"]], whole.at[k, me["ta"]])
+
+    def came(k, stage, p, off, ref):
+        sum_copy(k, stage, p, off, ("ta", "xy", "ta")[stage], ref, ref).wait_recv()
 
     def sum_start(k, matrix):
         row, col = iotas(half)
@@ -111,32 +111,36 @@
         flat = jnp.concatenate([mixed, matrix[half:, :half], tail], axis=0)
         for i in range(n_ta):
             packed[k, i] = flat[i * rows:(i + 1) * rows]
-        for off in range(1, n_ta):
-            scatter(k, off).start()
+        for p in range(PARTS):
+            for off in range(1, n_ta):
+                scatter(k, p, off).start()
 
     def sum_spread(k):
-        value = packed[k, me["ta"]]
-        for off in range(1, n_ta):
-            came(0, k, off, parts.at[k, off]).wait_recv()
-            value = value + parts[k, off]
-        total[k] = value
-        for off in range(1, n_xy):
-            spread(k, off).start()
+        for p, here in enumerate(parts_of):
+            value = packed[k, me["ta"], here]
+            for off in range(1, n_ta):
+                came(k, 0, p, off, parts.at[k, off])
+                value = value + parts[k, off, here]
+            total[k, here] = value
+            for off in range(1, n_xy):
+                spread(k, p, off).start()
 
     def sum_gather(k):
-        for off in range(1, n_xy):
-            came(1, k, off, planes.at[k, peer("xy", -off)]).wait_recv()
-        planes[k, me["xy"]] = total[k]
-        value = planes[k, 0]
-        for i in range(1, n_xy):
-            value = value + planes[k, i]
-        whole[k, me["ta"]] = value
-        for off in range(1, n_ta):
-            gather(k, off).start()
+        for p, here in enumerate(parts_of):
+            for off in range(1, n_xy):
+                came(k, 1, p, off, planes.at[k, peer("xy", -off)])
+            planes[k, me["xy"], here] = total[k, here]
+            value = planes[k, 0, here]
+            for i in range(1, n_xy):
+                value = value + planes[k, i, here]
+            whole[k, me["ta"], here] = value
+            for off in range(1, n_ta):
+                gather(k, p, off).start()
 
     def sum_done(k):
-        for off in range(1, n_ta):
-            came(2, k, off, whole.at[k, peer("ta", -off)]).wait_recv()
+        for p in range(PARTS):
+            for off in range(1, n_ta):
+                came(k, 2, p, off, whole.at[k, peer("ta", -off)])
         flat = jnp.concatenate([whole[k, i] for i in range(n_ta)], axis=0)
         row, col = iotas(half)
         mixed, low = flat[:half], flat[half:rhs]
@@ -148,11 +152,12 @@
                                 jnp.concatenate([low, last], axis=1)], axis=0)
 
     def sum_waits(k):
-        for off in range(1, n_ta):
-            scatter(k, off).wait_send()
-            gather(k, off).wait_send()
-        for off in range(1, n_xy):
-            spread(k, off).wait_send()
+        for p in range(PARTS):
+            for off in range(1, n_ta):
+                scatter(k, p, off).wait_send()
+                gather(k, p, off).wait_send()
+            for off in range(1, n_xy):
+                spread(k, p, off).wait_send()
 
     def gram(a, b):
         a, b = (v.reshape(-1, rhs) for v in (a, b))
@@ -236,7 +241,7 @@
         @pl.loop(0, per)
         def _(j):
             s = c * per + j
-            value = apply_far(s, halo1)
+            value = apply_far(s, halo)
             here, low = split(value)
             full[s] = value
             image[s] = here
@@ -279,11 +284,12 @@
             normal[s] = value
             rounded[s] = value.astype(bf16)
 
+    def residual(c):
+        value, high = normal[sites(c)], rounded[sites(c)]
+        return r[sites(c)].astype(f32) - times(high, (value - high.astype(f32)).astype(bf16), 0)
+
     def third(c):
-        value, high = normal[sites(c)], rounded[sites(c)]
-        here = r[sites(c)].astype(f32) - times(high, (value - high.astype(f32)).astype(bf16), 0)
-        residual[sites(c)] = here
-        gram_add(*split(here))
+        gram_add(*split(residual(c)))
 
     ahead = CHUNKS - 2
     for c in range(ahead):
@@ -318,24 +324,28 @@
             copy.wait_send()
 
     def fourth(c):
-        arrive(2, c)
-
-        @pl.loop(0, per)
-        def _(j):
-            s = c * per + j
-            acc[s] = apply_far(s, halo3)
+        for dirs in ((0, 1), (2,), (3,)) if c == CHUNKS - 1 else ((0, 1, 2, 3),):
+            for d in dirs:
+                vector_copy(2, d, c, rounded, halo).wait_recv()
+            for j in range(per):
+                s = c * per + j
+                total = acc[s]
+                for d in dirs:
+                    total = total + mul(lk[d + 1, s], halo[d, s], STRAIGHT)
+                acc[s] = total
 
         here = (full[sites(c)] - times(*split(acc[sites(c)]), 0)).astype(bf16)
         gram_ref[...] += gram(here, here)
 
     def fifth(c):
-        normal[sites(c)] = source_times(c, 0)
-        high, low = split(residual[sites(c)] + source_times(c, 1))
+        high, low = split(residual(c) + source_times(c, 1))
         u_out[0, sites(c)] = high
         u_out[1, sites(c)] = low
-
+        normal[sites(c)] = source_times(c, 0)
+
+    front, back = pl.ds(0, n // 2), pl.ds(n // 2, n // 2)
     outs = [pltpu.make_async_copy(source, target, local_sem.at[2 + k]) for k, (source, target) in enumerate(
-        ((normal, first_ref), (u_out.at[0], high_ref), (u_out.at[1], low_ref)))]
+        ((normal.at[front], first_ref), (normal.at[back], second_ref), (u_out.at[0], high_ref), (u_out.at[1], low_ref)))]
     begin = EARLY[2] + 1
     for c in range(CHUNKS):
         fourth(c)
@@ -384,19 +394,19 @@
     square = lambda *lead: pltpu.VMEM(lead + (rhs, rhs), f32)
     return pl.pallas_call(
         functools.partial(krylov_kernel, sizes, ny, nz),
-        out_shape=[jax.ShapeDtypeStruct((n, comp, rhs), d) for d in (f32, bf16, bf16)]
+        out_shape=[jax.ShapeDtypeStruct((n // 2, comp, rhs), f32)] * 2 + [jax.ShapeDtypeStruct((n, comp, rhs), bf16)] * 2
         + [jax.ShapeDtypeStruct((rhs, rhs), f32)] * 2,
         in_specs=[anywhere, anywhere],
-        out_specs=[anywhere] * 3 + [vmem] * 2,
+        out_specs=[anywhere] * 4 + [vmem] * 2,
         scratch_shapes=[
-            slab(), pltpu.VMEM((links.shape[0], n, comp, comp), bf16), slab(4), slab(4), slab(4), slab(4), slab(), slab(),
-            wide, wide, wide, wide, square(), square(), square(2), square(), square(2), pltpu.VMEM((4, rhs, rhs), bf16),
+            slab(), pltpu.VMEM((links.shape[0], n, comp, comp), bf16), slab(4), slab(4), slab(4), slab(), slab(),
+            wide, wide, wide, square(), square(), square(2), square(), square(2), pltpu.VMEM((4, rhs, rhs), bf16),
             pieces(n_ta), pieces(n_ta), pltpu.VMEM((SUMS, rows, rhs // 2), f32), pieces(n_xy), pieces(n_ta),
-            pltpu.SemaphoreType.DMA((5,)), pltpu.SemaphoreType.DMA((3, 4, CHUNKS)), pltpu.SemaphoreType.DMA((3, 4, CHUNKS)),
-            pltpu.SemaphoreType.DMA((SUMS, 3, most)), pltpu.SemaphoreType.DMA((SUMS, 3, most)),
+            pltpu.SemaphoreType.DMA((6,)), pltpu.SemaphoreType.DMA((3, 4, CHUNKS)), pltpu.SemaphoreType.DMA((3, 4, CHUNKS)),
+            pltpu.SemaphoreType.DMA((SUMS, 3, PARTS, most)), pltpu.SemaphoreType.DMA((SUMS, 3, PARTS, most)),
         ],
         cost_estimate=pl.CostEstimate(flops=int(6e9), bytes_accessed=64 << 20, transcendentals=0),
-        compiler_params=pltpu.CompilerParams(collective_id=0, has_side_effects=True, vmem_limit_bytes=67043328),
+        compiler_params=pltpu.CompilerParams(collective_id=0, has_side_effects=True, vmem_limit_bytes=46 << 20),
     )(sources.reshape(n, comp, rhs), links.reshape(links.shape[0], n, comp, comp))
 
 
@@ -484,48 +494,42 @@
         out_ref[...] = solved(s_ref[...], x, right) * down
 
 
-def closing_kernel(chunks, curvature_ref, fresh_ref, first_hbm, high_hbm, low_hbm, out_hbm,
-                   first, high, low, coef, x_ref, s_ref, alpha_ref, load_sem, store_sem):
-    n, comp, rhs = first.shape
+def closing_kernel(chunks, curvature_ref, fresh_ref, first, second, high, low, out_hbm, out, coef, x_ref, s_ref, alpha_ref, store_sem):
+    n, comp, rhs = high.shape
     per = n // chunks
-    loads = [pltpu.make_async_copy(source, target, load_sem.at[k]) for k, (source, target) in enumerate(
-        ((first_hbm, first), (high_hbm, high), (low_hbm, low)))]
-    for copy in loads:
-        copy.start()
     solve(curvature_ref[...], fresh_ref[...], x_ref, s_ref, alpha_ref)
     coef[0], coef[1] = split(alpha_ref[...])
-    for copy in loads:
-        copy.wait()
 
     def store(c):
-        return pltpu.make_async_copy(first.at[pl.ds(c * per, per)], out_hbm.at[pl.ds(c * per, per)], store_sem.at[c])
-
-    @pl.loop(0, chunks)
-    def _(c):
-        here = pl.ds(c * per, per)
-        left, rest = high[here].reshape(-1, rhs), low[here].reshape(-1, rhs)
-        step = mul(left, coef[0], STRAIGHT) + mul(left, coef[1], STRAIGHT) + mul(rest, coef[0], STRAIGHT)
-        first[here] = first[here] + step.reshape(per, comp, rhs)
-        store(c).start()
+        return pltpu.make_async_copy(out.at[pl.ds(c * per, per)], out_hbm.at[pl.ds(c * per, per)], store_sem.at[c])
+
+    for base, lo in ((first, 0), (second, chunks // 2)):
+        @pl.loop(0, chunks // 2)
+        def _(c):
+            here = pl.ds((lo + c) * per, per)
+            left, rest = high[here].reshape(-1, rhs), low[here].reshape(-1, rhs)
+            step = mul(left, coef[0], STRAIGHT) + mul(left, coef[1], STRAIGHT) + mul(rest, coef[0], STRAIGHT)
+            out[here] = base[pl.ds(c * per, per)] + step.reshape(per, comp, rhs)
+            store(lo + c).start()
 
     @pl.loop(0, chunks)
     def _(c):
         store(c).wait()
 
 
-def closing(first, high, low, curvature, fresh):
+def closing(first, second, high, low, curvature, fresh):
     vmem, anywhere = pl.BlockSpec(memory_space=pltpu.VMEM), pl.BlockSpec(memory_space=pl.ANY)
     rhs = fresh.shape[0]
     return pl.pallas_call(
         functools.partial(closing_kernel, CHUNKS),
-        out_shape=jax.ShapeDtypeStruct(first.shape, f32),
-        in_specs=[vmem] * 2 + [anywhere] * 3,
+        out_shape=jax.ShapeDtypeStruct(high.shape, f32),
+        in_specs=[vmem] * 6,
         out_specs=anywhere,
-        scratch_shapes=[pltpu.VMEM(first.shape, f32), pltpu.VMEM(first.shape, bf16), pltpu.VMEM(first.shape, bf16),
-                        pltpu.VMEM((2, rhs, rhs), bf16)] + [pltpu.VMEM((rhs, rhs), f32)] * 3
-        + [pltpu.SemaphoreType.DMA((3,)), pltpu.SemaphoreType.DMA((CHUNKS,))],
+        scratch_shapes=[pltpu.VMEM(high.shape, f32), pltpu.VMEM((2, rhs, rhs), bf16)] + [pltpu.VMEM((rhs, rhs), f32)] * 3
+        + [pltpu.SemaphoreType.DMA((CHUNKS,))],
         cost_estimate=pl.CostEstimate(flops=int(4e9), bytes_accessed=10 << 20, transcendentals=0),
-    )(curvature, fresh, first, high, low)
+        compiler_params=pltpu.CompilerParams(vmem_limit_bytes=20 << 20),
+    )(curvature, fresh, first, second, high, low)
 
 
 def solution(mesh):

time: 278 us -> 277 us (level)
  no operation moved by 1% of the time
where the time goes in v3:
time: 277 us
  Pallas kernels  276 us (100%)
    pallas_call x1, Pallas kernels, krylov(): pl.pallas_call(functools.partial(krylov_kernel, sizes, ny, nz), out_shape...  234 us
    pallas_call x1, Pallas kernels, closing(): pl.pallas_call(functools.partial(closing_kernel, CHUNKS), out_shape=jax.S...  42.2 us

profile of v3, /device:TPU:0, one launch (start us, length us, event | category | flops | bytes accessed | tf_op | source)
XLA Modules:
  0.0 276.7 jit_solution(3669903074165807274)
XLA Ops:
  0.0 234.3 %shard_map.28 = (f32[16,96,256]{2,1,0:T(8,128)S(1)}, f32[16,96,256]{2,1,0:T(8,128)S(1)}, bf16[32,96,256]{2,1,0:T(8,128)(2,1)S(1)}, bf16[32,96,256]{2,1,0:T(8,128...) custom-call(bf16[32,96,256]{2,1,0:T(8,128)(2,1)} %bitcast.6, bf16[9,32,96,96]{3,2,1,0:T(8,128)(2,1)} %bitcast.5), custom_call_target="tpu_custom_call" | custom-call | flops 6000000000 | bytes 67108864 | tf_op jit(solution)/shard_map/pallas_call | solution.py:395
  234.3 42.2 %shard_map.29 = f32[32,96,256]{2,1,0:T(8,128)} custom-call(f32[256,256]{1,0:T(8,128)S(1)} %get-tuple-element.11.curvature_ref, f32[256,256]{1,0:T(8,128)S(1)} %get-tuple-element.12.fresh_ref, f32[16,96,256]{2,1,0:T(8,128)S(1)} %get-tuple-element.13.first, f32[16,96,256]{2,1,0:T(8,128)S(1)} %get-tuple-element.14.second, ...), custom_call_target="tpu_custom_call" | custom-call | flops 4000000000 | bytes 10485760 | tf_op jit(solution)/shard_map/pallas_call | solution.py:523

commit v4 on v3

--- a/solution.py
+++ b/solution.py
@@ -17,7 +17,7 @@
 CHUNKS = 8
 EARLY = (2, 3, 4)
 SUMS = 4
-PARTS = 3
+PARTS = 1
 
 mul = functools.partial(lax.dot_general, preferred_element_type=f32)
 STRAIGHT = (((1,), (0,)), ((), ()))
@@ -62,15 +62,21 @@
             send_sem=bulk_send.at[1, d, c], recv_sem=bulk_recv.at[1, d, c],
             device_id={axis: peer(axis, step)}, device_id_type=MESH)
 
-    def copies(stage, c):
-        if stage == 0:
-            return [vector_copy(0, d, c, src, halo) for d in (3, 2, 1, 0)]
+    def copies(stage, c, dirs=(3, 2, 1, 0)):
         if stage == 1:
-            return [product_copy(d, c) for d in (3, 2, 1, 0)]
-        return [vector_copy(2, d, c, rounded, halo) for d in (3, 2, 1, 0)]
+            return [product_copy(d, c) for d in dirs]
+        return [vector_copy(stage, d, c, rounded if stage else src, halo) for d in dirs]
 
     def send(stage, c):
-        for copy in copies(stage, c):
+        last = (me["xy"] + 1) // n_xy
+        first = (2 + last, 3 - last, 2 + last)[stage]
+        source, target = ((src, halo), (u_out, u_in), (rounded, halo))[stage]
+        for d, step in ((first, 2 * last - 1), (5 - first, 1 - 2 * last)):
+            pltpu.make_async_remote_copy(
+                src_ref=source.at[d, sites(c)] if stage == 1 else source.at[sites(c)], dst_ref=target.at[d, sites(c)],
+                send_sem=bulk_send.at[stage, d, c], recv_sem=bulk_recv.at[stage, d, c],
+                device_id={"xy": peer("xy", step)}, device_id_type=MESH).start()
+        for copy in copies(stage, c, (1, 0)):
             copy.start()
 
     def send_range(stage, lo, hi):

time: 277 us -> 274 us (0.989)
  no operation moved by 1% of the time
where the time goes in v4:
time: 274 us
  Pallas kernels  274 us (100%)
    pallas_call x1, Pallas kernels, krylov(): pl.pallas_call(functools.partial(krylov_kernel, sizes, ny, nz), out_shape...  232 us
    pallas_call x1, Pallas kernels, closing(): pl.pallas_call(functools.partial(closing_kernel, CHUNKS), out_shape=jax.S...  42.2 us

profile of v4, /device:TPU:0, one launch (start us, length us, event | category | flops | bytes accessed | tf_op | source)
XLA Modules:
  0.0 274.2 jit_solution(2093057020988888517)
XLA Ops:
  0.0 231.8 %shard_map.28 = (f32[16,96,256]{2,1,0:T(8,128)S(1)}, f32[16,96,256]{2,1,0:T(8,128)S(1)}, bf16[32,96,256]{2,1,0:T(8,128)(2,1)S(1)}, bf16[32,96,256]{2,1,0:T(8,128...) custom-call(bf16[32,96,256]{2,1,0:T(8,128)(2,1)} %bitcast.6, bf16[9,32,96,96]{3,2,1,0:T(8,128)(2,1)} %bitcast.5), custom_call_target="tpu_custom_call" | custom-call | flops 6000000000 | bytes 67108864 | tf_op jit(solution)/shard_map/pallas_call | solution.py:401
  231.8 42.2 %shard_map.29 = f32[32,96,256]{2,1,0:T(8,128)} custom-call(f32[256,256]{1,0:T(8,128)S(1)} %get-tuple-element.11.curvature_ref, f32[256,256]{1,0:T(8,128)S(1)} %get-tuple-element.12.fresh_ref, f32[16,96,256]{2,1,0:T(8,128)S(1)} %get-tuple-element.13.first, f32[16,96,256]{2,1,0:T(8,128)S(1)} %get-tuple-element.14.second, ...), custom_call_target="tpu_custom_call" | custom-call | flops 4000000000 | bytes 10485760 | tf_op jit(solution)/shard_map/pallas_call | solution.py:529

commit v5 on v4

--- a/solution.py
+++ b/solution.py
@@ -527,7 +527,7 @@
     vmem, anywhere = pl.BlockSpec(memory_space=pltpu.VMEM), pl.BlockSpec(memory_space=pl.ANY)
     rhs = fresh.shape[0]
     return pl.pallas_call(
-        functools.partial(closing_kernel, CHUNKS),
+        functools.partial(closing_kernel, CHUNKS // 2),
         out_shape=jax.ShapeDtypeStruct(high.shape, f32),
         in_specs=[vmem] * 6,
         out_specs=anywhere,

time: 274 us -> 274 us (level)
  no operation moved by 1% of the time
where the time goes in v5:
time: 274 us
  Pallas kernels  273 us (100%)
    pallas_call x1, Pallas kernels, krylov(): pl.pallas_call(functools.partial(krylov_kernel, sizes, ny, nz), out_shape...  232 us
    pallas_call x1, Pallas kernels, closing(): pl.pallas_call(functools.partial(closing_kernel, CHUNKS // 2), out_shape=...  41.6 us

profile of v5, /device:TPU:0, one launch (start us, length us, event | category | flops | bytes accessed | tf_op | source)
XLA Modules:
  0.0 273.6 jit_solution(1203880706554659421)
XLA Ops:
  0.0 231.8 %shard_map.28 = (f32[16,96,256]{2,1,0:T(8,128)S(1)}, f32[16,96,256]{2,1,0:T(8,128)S(1)}, bf16[32,96,256]{2,1,0:T(8,128)(2,1)S(1)}, bf16[32,96,256]{2,1,0:T(8,128...) custom-call(bf16[32,96,256]{2,1,0:T(8,128)(2,1)} %bitcast.6, bf16[9,32,96,96]{3,2,1,0:T(8,128)(2,1)} %bitcast.5), custom_call_target="tpu_custom_call" | custom-call | flops 6000000000 | bytes 67108864 | tf_op jit(solution)/shard_map/pallas_call | solution.py:401
  231.8 41.6 %shard_map.29 = f32[32,96,256]{2,1,0:T(8,128)} custom-call(f32[256,256]{1,0:T(8,128)S(1)} %get-tuple-element.11.curvature_ref, f32[256,256]{1,0:T(8,128)S(1)} %get-tuple-element.12.fresh_ref, f32[16,96,256]{2,1,0:T(8,128)S(1)} %get-tuple-element.13.first, f32[16,96,256]{2,1,0:T(8,128)S(1)} %get-tuple-element.14.second, ...), custom_call_target="tpu_custom_call" | custom-call | flops 4000000000 | bytes 10485760 | tf_op jit(solution)/shard_map/pallas_call | solution.py:529
